TPU v7x, 512 devices: a whole 4x4x16 slice. The times are simulated.
512 devices in a mesh: src: 4 (over y), seq: 8 (over z_hi, core), head: 16 (over z_lo, x).
Axes of the slice: x: 4, y: 4, z: 16 (z_hi: 4, z_lo: 4; z = z_hi * 4 + z_lo), core: 2. Of those that a mesh axis runs over, the one named last changes fastest.
Arguments:
- enc_out: bfloat16 [32768, 4096], P(('src', 'seq'), 'head'), parts along dimension 0, may hold values from -9 to 9
- enc_gain: float32 [4096], replicated, may hold values from 0.25 to 1.75
- key_weight: bfloat16 [4096, 4096], P('seq', 'head'), may hold values from -1 to 1
- value_weight: bfloat16 [4096, 4096], P('seq', 'head'), may hold values from -0.09375 to 0.09375
- query_weight: bfloat16 [4096, 4096], P('seq', 'head'), may hold values from -2 to 2
- out_weight: bfloat16 [4096, 4096], P('head', 'seq'), may hold values from -0.09375 to 0.09375
- dec_gain: float32 [4096], replicated, may hold values from 0.25 to 1.75
- beam_state: float32 [64, 4096], P('src'), parts along dimension 0, may hold values from -7 to 7
- parents: int32 [8, 16], P('src'), parts along dimension 0, may hold values from 0 to 15
- token_embed: bfloat16 [8, 16, 4096], P('src'), parts along dimension 0, may hold values from -6 to 6
Outputs:
- final_state: float32 [64, 4096], P('src'), parts along dimension 0
- attended: float32 [64, 4096], P('src'), parts along dimension 0
There are 4 independent parts, one for each index of `src`. A program takes and returns all parts, laid end to end along the dimension named above; an argument that names none is the same for every part. Nothing has to cross between parts.
All inputs are finite; a program needn't handle non-finite values.
Results may differ from a plain program's by a relative error of at most 0.013.
The roundings to bfloat16 on the way count: a program that leaves them out, or rounds other values in their place, can miss the bound.
Values may be sent and summed in bfloat16 or wider, within the bound.
A program may use at most 64 MiB of HBM per device.

v0:
```python
import jax
import jax.numpy as jnp
from jax import lax
from jax.sharding import PartitionSpec as P

HEAD_DIM = 64
BEAMS = 16
STEPS = 2


def rms_norm(values, gain):
    mean_square = jnp.mean(values * values, axis=-1, keepdims=True)
    return values * lax.rsqrt(mean_square + 1e-06) * gain


def on_device(
    enc_out,
    enc_gain,
    key_weight,
    value_weight,
    query_weight,
    out_weight,
    dec_gain,
    beam_state,
    parents,
    token_embed,
):
    full_rows = lax.all_gather(enc_out, "head", axis=1, tiled=True)
    memory = rms_norm(full_rows.astype(jnp.float32), enc_gain).astype(jnp.bfloat16)
    key_full, value_full = (
        lax.all_gather(key_weight, "seq", axis=0, tiled=True),
        lax.all_gather(value_weight, "seq", axis=0, tiled=True),
    )
    rows = memory.shape[0]
    heads_here = key_weight.shape[1] // HEAD_DIM
    keys = jnp.dot(memory, key_full, preferred_element_type=jnp.float32).astype(jnp.bfloat16)
    values = jnp.dot(memory, value_full, preferred_element_type=jnp.float32).astype(jnp.bfloat16)
    keys = keys.reshape(rows, heads_here, HEAD_DIM)
    values = values.reshape(rows, heads_here, HEAD_DIM)
    feat_rows = query_weight.shape[0]
    feat_start = lax.axis_index("seq") * feat_rows
    state = beam_state
    attended = jnp.zeros(beam_state.shape, jnp.float32)
    for step in range(STEPS):
        state = jnp.take(state, parents[step], axis=0) + token_embed[step].astype(jnp.float32)
        normed = rms_norm(state, dec_gain).astype(jnp.bfloat16)
        normed_part = lax.dynamic_slice_in_dim(normed, feat_start, feat_rows, 1)
        query_part = jnp.dot(normed_part, query_weight, preferred_element_type=jnp.float32)
        query = lax.psum(query_part, "seq").astype(jnp.bfloat16)
        query = query.reshape(BEAMS, heads_here, HEAD_DIM)
        scores = jnp.einsum("bhd,shd->bhs", query, keys, preferred_element_type=jnp.float32) * 0.125
        top = jnp.max(scores, axis=-1)
        expo = jnp.exp(scores - top[..., None])
        total = jnp.sum(expo, axis=-1)
        weights = expo.astype(jnp.bfloat16)
        weighted = jnp.einsum("bhs,shd->bhd", weights, values, preferred_element_type=jnp.float32)
        peak_all = lax.pmax(top, "seq")
        factor = jnp.exp(top - peak_all)
        total_all, weighted_all = lax.psum((total * factor, weighted * factor[..., None]), "seq")
        context = (weighted_all / total_all[..., None]).astype(jnp.bfloat16)
        context = context.reshape(BEAMS, heads_here * HEAD_DIM)
        partial_out = jnp.dot(context, out_weight, preferred_element_type=jnp.float32)
        columns = lax.psum(partial_out.astype(jnp.bfloat16), "head").astype(jnp.float32)
        added = lax.all_gather(columns.astype(jnp.bfloat16), "seq", axis=1, tiled=True).astype(
            columns.dtype
        )
        state = state + added
        attended = attended + added
    return (state, attended)


def solution(mesh):
    placed = (
        P(("src", "seq"), "head"),
        P(),
        P("seq", "head"),
        P("seq", "head"),
        P("seq", "head"),
        P("head", "seq"),
        P(),
        P("src", None),
        P("src", None),
        P("src", None, None),
    )
    return jax.shard_map(
        on_device,
        mesh=mesh,
        in_specs=placed,
        out_specs=(P("src", None), P("src", None)),
        check_vma=False,
    )
```

profile of v0, /device:TPU:9, one launch (start us, length us, event | category | flops | bytes accessed | tf_op | source)
XLA Modules:
  0.0 602.1 jit_solution(18296726417365405977)
XLA Ops:
  7.2 0.7 all-gather.4.cloned.1.call-update
  8.0 0.7 all-gather.8.cloned.1.call-update
  8.7 0.7 all-gather.6.cloned.1.call-update
  9.4 0.8 compare_and_fusion
  10.8 0.8 dynamic-slice
  11.6 1.1 multiply_reduce_fusion.1
  12.7 1.1 fusion.29
  13.9 40.7 %psum.56 = bf16[16,256]{1,0:T(8,128)(2,1)S(1)} all-reduce(f32[16,256]{1,0:T(8,128)S(1)} %fusion.29), channel_id=1, replica_groups=mesh['src'=4,'seq'=8,'head'=16] {'seq'}, use_global_device_ids=true, to_apply=%region_2.4 | all-reduce | flops 4096 | bytes 24576 | tf_op jit(solution)/shard_map/psum | solution.py:49
  54.6 78.1 %all-gather.4.cloned.1.call-done = bf16[1024,4096]{1,0:T(8,128)(2,1)} async-done(((bf16[1024,256]{1,0:T(8,128)(2,1)}), bf16[1024,4096]{1,0:T(8,128)(2,1)}) %all-gather.4.cloned.1.call-update) | async-done | bytes 8388624 | tf_op jit(solution)/shard_map/all_gather | solution.py:28
  132.8 5.1 fusion
  137.8 70.8 %all-gather.8.cloned.1.call-done = bf16[4096,256]{1,0:T(8,128)(2,1)} async-done(((bf16[512,256]{1,0:T(8,128)(2,1)}), bf16[4096,256]{1,0:T(8,128)(2,1)}) %all-gather.8.cloned.1.call-update) | async-done | bytes 2097168 | tf_op jit(solution)/shard_map/all_gather | solution.py:31
  208.6 6.6 %fusion.10 = bf16[1024,256]{0,1:T(8,128)(2,1)S(1)} fusion(bf16[4096,256]{1,0:T(8,128)(2,1)} %all-gather.8.cloned.1.call-done, bf16[1024,4096]{1,0:T(8,128)(2,1)} %all-gather.4.cloned.1.call-done, f32[4096]{0:T(1024)S(1)} %copy-done.4, f32[1024]{0:T(1024)S(1)} %add_rsqrt_fusion), kind=kOutput, calls=%fused_computation.10 | convolution fusion | flops 2164523008 | bytes 11030528 | tf_op jit(solution)/shard_map/dot_general | solution.py:36
  215.5 21.9 %pmax.14 = f32[16,4]{0,1:T(4,128)S(1)} all-reduce(f32[16,4]{0,1:T(4,128)S(1)} %get-tuple-element.23), channel_id=1, replica_groups=mesh['src'=4,'seq'=8,'head'=16] {'seq'}, use_global_device_ids=true, to_apply=%region_4.6 | all-reduce | flops 64 | bytes 512 | tf_op jit(solution)/shard_map/pmax | solution.py:57
  237.6 28.6 %all-gather.6.cloned.1.call-done = bf16[4096,256]{1,0:T(8,128)(2,1)} async-done(((bf16[512,256]{1,0:T(8,128)(2,1)}), bf16[4096,256]{1,0:T(8,128)(2,1)}) %all-gather.6.cloned.1.call-update) | async-done | bytes 2097168 | tf_op jit(solution)/shard_map/all_gather | solution.py:32
  266.2 6.6 %fusion.7 = bf16[1024,256]{0,1:T(8,128)(2,1)S(1)} fusion(bf16[4096,256]{1,0:T(8,128)(2,1)} %all-gather.6.cloned.1.call-done, bf16[1024,4096]{1,0:T(8,128)(2,1)} %all-gather.4.cloned.1.call-done, f32[4096]{0:T(1024)S(1)} %copy-done.4, f32[1024]{0:T(1024)S(1)} %add_rsqrt_fusion), kind=kOutput, calls=%fused_computation.9 | convolution fusion | flops 2164523008 | bytes 11030528 | tf_op jit(solution)/shard_map/dot_general | solution.py:37
  273.1 34.6 %all-reduce.1 = (f32[16,4,64]{2,0,1:T(8,128)S(1)}, f32[16,4]{0,1:T(4,128)S(1)}) all-reduce(f32[16,4,64]{2,0,1:T(8,128)S(1)} %fusion.16, f32[16,4]{0,1:T(4,128)S(1)} %get-tuple-element.13), channel_id=1, replica_groups=mesh['src'=4,'seq'=8,'head'=16] {'seq'}, use_global_device_ids=true, to_apply=%region_5.7 | all-reduce | flops 4160 | bytes 33280 | tf_op jit(solution)/shard_map/psum | solution.py:59
  308.0 64.0 %psum.59 = bf16[16,512]{1,0:T(8,128)(2,1)S(1)} all-reduce(bf16[16,512]{1,0:T(8,128)(2,1)S(1)} %convolution_convert_fusion.1), channel_id=1, replica_groups=mesh['src'=4,'seq'=8,'head'=16] {'head'}, use_global_device_ids=true, to_apply=%region_8.10 | all-reduce | flops 8192 | bytes 32768 | tf_op jit(solution)/shard_map/psum | solution.py:63
  372.1 35.7 %all_gather.18 = bf16[16,4096]{1,0:T(8,128)(2,1)S(1)} all-gather(bf16[16,512]{1,0:T(8,128)(2,1)S(1)} %psum.59), channel_id=1, replica_groups=mesh['src'=4,'seq'=8,'head'=16] {'seq'}, dimensions={1}, use_global_device_ids=true | all-gather | bytes 147456 | tf_op jit(solution)/shard_map/all_gather | solution.py:64
  408.9 33.7 %psum.60 = bf16[16,256]{1,0:T(8,128)(2,1)S(1)} all-reduce(f32[16,256]{1,0:T(8,128)S(1)} %fusion.31), channel_id=1, replica_groups=mesh['src'=4,'seq'=8,'head'=16] {'seq'}, use_global_device_ids=true, to_apply=%region_10.12 | all-reduce | flops 4096 | bytes 24576 | tf_op jit(solution)/shard_map/psum | solution.py:49
  443.0 20.1 %pmax.15 = f32[16,4]{0,1:T(4,128)S(1)} all-reduce(f32[16,4]{0,1:T(4,128)S(1)} %get-tuple-element.25), channel_id=1, replica_groups=mesh['src'=4,'seq'=8,'head'=16] {'seq'}, use_global_device_ids=true, to_apply=%region_12.14 | all-reduce | flops 64 | bytes 512 | tf_op jit(solution)/shard_map/pmax | solution.py:57
  463.6 35.0 %all-reduce = (f32[16,4,64]{2,0,1:T(8,128)S(1)}, f32[16,4]{0,1:T(4,128)S(1)}) all-reduce(f32[16,4,64]{2,0,1:T(8,128)S(1)} %fusion.15, f32[16,4]{0,1:T(4,128)S(1)} %get-tuple-element.7), channel_id=1, replica_groups=mesh['src'=4,'seq'=8,'head'=16] {'seq'}, use_global_device_ids=true, to_apply=%region_13.15 | all-reduce | flops 4160 | bytes 33280 | tf_op jit(solution)/shard_map/psum | solution.py:59
  498.9 60.6 %psum.63 = bf16[16,512]{1,0:T(8,128)(2,1)S(1)} all-reduce(bf16[16,512]{1,0:T(8,128)(2,1)S(1)} %convolution_convert_fusion), channel_id=1, replica_groups=mesh['src'=4,'seq'=8,'head'=16] {'head'}, use_global_device_ids=true, to_apply=%region_16.18 | all-reduce | flops 8192 | bytes 32768 | tf_op jit(solution)/shard_map/psum | solution.py:63
  559.5 35.3 %all_gather.19 = bf16[16,4096]{1,0:T(8,128)(2,1)S(1)} all-gather(bf16[16,512]{1,0:T(8,128)(2,1)S(1)} %psum.63), channel_id=1, replica_groups=mesh['src'=4,'seq'=8,'head'=16] {'seq'}, dimensions={1}, use_global_device_ids=true | all-gather | bytes 147456 | tf_op jit(solution)/shard_map/all_gather | solution.py:64
  594.8 0.8 convert_add_fusion
  (41 shorter events, 4.2 us)
Async XLA Ops:
  7.2 3.0 copy-start
  7.2 201.4 %copy-start.4 = (f32[4096]{0:T(1024)S(1)}, f32[4096]{0:T(1024)}, u32[]{:S(2)}) copy-start(f32[4096]{0:T(1024)} %param.13) | copy-start | bytes 49156
  7.2 125.6 %all-gather.4.cloned.1.call-start = ((), (), s32[]{:S(2)}) async-start(), calls=%async_computation | async-start | bytes 8912896 | tf_op jit(solution)/shard_map/all_gather | solution.py:28
  7.9 200.7 %all-gather.8.cloned.1.call-start = ((), (), s32[]{:S(2)}) async-start(), calls=%async_computation.2 | async-start | bytes 2359296 | tf_op jit(solution)/shard_map/all_gather | solution.py:31
  8.7 257.5 %all-gather.6.cloned.1.call-start = ((), (), s32[]{:S(2)}) async-start(), calls=%async_computation.1 | async-start | bytes 2359296 | tf_op jit(solution)/shard_map/all_gather | solution.py:32
  237.6 70.3 %copy-start.2 = (bf16[256,512]{1,0:T(8,128)(2,1)S(1)}, bf16[256,512]{1,0:T(8,128)(2,1)}, u32[]{:S(2)}) copy-start(bf16[256,512]{1,0:T(8,128)(2,1)} %param.17) | copy-start | bytes 786436
  237.6 170.9 %copy-start.3 = (bf16[2,16,4096]{2,1,0:T(8,128)(2,1)S(1)}, bf16[2,16,4096]{2,1,0:T(8,128)(2,1)}, u32[]{:S(2)}) copy-start(bf16[2,16,4096]{2,1,0:T(8,128)(2,1)} %param.21) | copy-start | bytes 786436
  237.6 171.1 %copy-start.1 = (bf16[512,256]{1,0:T(8,128)(2,1)S(1)}, bf16[512,256]{1,0:T(8,128)(2,1)}, u32[]{:S(2)}) copy-start(bf16[512,256]{1,0:T(8,128)(2,1)} %param.16) | copy-start | bytes 786436
Sparse Core Ops, SparseCore 0:
  10.0 122.7 all-gather.3
  134.9 73.6 all-gather.7
  210.8 55.3 all-gather.5
where the time goes:
time: 603 us; the launch traced here: 602 us
  blocking collectives  382 us (63%)
  waiting for transfers between devices  180 us (30%)
  matrix products  15.9 us (3%)
  between operations  13.9 us (2%)
  other arithmetic  8.64 us (1%)
    psum x2, blocking collectives, on_device(): lax.psum(partial_out.astype(jnp.bfloat16), 'head').astype(jnp.float32)  125 us
    all_gather x1, waiting for transfers between devices, on_device(): full_rows = lax.all_gather(enc_out, 'head', axis=1, tiled=True)  78.1 us
    psum x2, blocking collectives, on_device(): query = lax.psum(query_part, 'seq').astype(jnp.bfloat16)  74.3 us
    all_gather x2, blocking collectives, on_device(): lax.all_gather(columns.astype(jnp.bfloat16), 'seq', axis=1, tiled=True)  71 us
    all_gather x1, waiting for transfers between devices, on_device(): lax.all_gather(key_weight, 'seq', axis=0, tiled=True)  70.8 us
    psum x2, blocking collectives, on_device(): lax.psum((total * factor, weighted * factor[..., None]), 'seq')  69.6 us
    pmax x2, blocking collectives, on_device(): peak_all = lax.pmax(top, 'seq')  42 us
    all_gather x1, waiting for transfers between devices, on_device(): lax.all_gather(value_weight, 'seq', axis=0, tiled=True)  28.6 us
  transfers between devices with their start and end apart: 3, of which 3 were waited for; matrix products, arithmetic and copies ran while one was open for 3% of the time, Pallas kernels for 0%

commit v1 on v0

--- a/solution.py
+++ b/solution.py
@@ -6,6 +6,13 @@
 HEAD_DIM = 64
 BEAMS = 16
 STEPS = 2
+
+
+def exchange_gather(x, axis, dim):
+    devices = lax.axis_size(axis)
+    tiles = jnp.stack([x for _ in range(devices)])
+    tiles = lax.all_to_all(tiles, axis, split_axis=0, concat_axis=0)
+    return jnp.concatenate(tiles, axis=dim)
 
 
 def rms_norm(values, gain):
@@ -28,7 +35,7 @@
     full_rows = lax.all_gather(enc_out, "head", axis=1, tiled=True)
     memory = rms_norm(full_rows.astype(jnp.float32), enc_gain).astype(jnp.bfloat16)
     key_full, value_full = (
-        lax.all_gather(key_weight, "seq", axis=0, tiled=True),
+        exchange_gather(key_weight, "seq", 0),
         lax.all_gather(value_weight, "seq", axis=0, tiled=True),
     )
     rows = memory.shape[0]

time: 603 us -> 626 us (1.038)
  blocking collectives: 382 us -> 472 us
  waiting for transfers between devices: 180 us -> 96.4 us
  starting transfers between devices: 0.11 us -> 15.9 us
    psum x2, blocking collectives: 74.3 us -> 156 us  [on_device(): query = lax.psum(query_part, 'seq').astype(jnp.bfloat16)]
    all_gather x1 -> x0, waiting for transfers between devices: 70.8 us -> none  [on_device(): lax.all_gather(key_weight, 'seq', axis=0, tiled=True)]
    all_to_all x0 -> x1, starting transfers between devices: none -> 15.9 us  [exchange_gather(): tiles = lax.all_to_all(tiles, axis, split_axis=0, concat_axis=0)]
    all_gather x1, waiting for transfers between devices: 78.1 us -> 66.7 us  [on_device(): full_rows = lax.all_gather(enc_out, 'head', axis=1, tiled=True)]
    pmax x2, blocking collectives: 42 us -> 50.1 us  [on_device(): peak_all = lax.pmax(top, 'seq')]
  transfers between devices with their start and end apart: 3 -> 3, of which waited for: 3 -> 2; matrix products, arithmetic and copies ran while one was open for 3% -> 3% of each run, Pallas kernels for 0% -> 0%
where the time goes in v1:
time: 626 us
  blocking collectives  472 us (75%)
  waiting for transfers between devices  96.4 us (15%)
  starting transfers between devices  15.9 us (3%)
  matrix products  14.6 us (2%)
  between operations  14.2 us (2%)
  other arithmetic  7.75 us (1%)
    psum x2, blocking collectives, on_device(): query = lax.psum(query_part, 'seq').astype(jnp.bfloat16)  156 us
    psum x2, blocking collectives, on_device(): lax.psum(partial_out.astype(jnp.bfloat16), 'head').astype(jnp.float32)  124 us
    all_gather x2, blocking collectives, on_device(): lax.all_gather(columns.astype(jnp.bfloat16), 'seq', axis=1, tiled=True)  71.6 us
    psum x2, blocking collectives, on_device(): lax.psum((total * factor, weighted * factor[..., None]), 'seq')  69.6 us
    all_gather x1, waiting for transfers between devices, on_device(): full_rows = lax.all_gather(enc_out, 'head', axis=1, tiled=True)  66.7 us
    pmax x2, blocking collectives, on_device(): peak_all = lax.pmax(top, 'seq')  50.1 us
    all_gather x1, waiting for transfers between devices, on_device(): lax.all_gather(value_weight, 'seq', axis=0, tiled=True)  28.3 us
    all_to_all x1, starting transfers between devices, exchange_gather(): tiles = lax.all_to_all(tiles, axis, split_axis=0, concat_axis=0)  15.9 us
  transfers between devices with their start and end apart: 3, of which 2 were waited for; matrix products, arithmetic and copies ran while one was open for 3% of the time, Pallas kernels for 0%

profile of v1, /device:TPU:9, one launch (start us, length us, event | category | flops | bytes accessed | tf_op | source)
XLA Modules:
  0.0 625.6 jit_solution(8986663522904140282)
XLA Ops:
  7.2 0.7 all-gather.3.cloned.1.call-update
  7.9 2.4 stack.2
  10.3 15.9 %all-to-all-start = ((bf16[8,512,256]{2,1,0:T(8,128)(2,1)}), bf16[8,512,256]{2,1,0:T(8,128)(2,1)S(1)}, u32[]{:S(2)}, u32[]{:S(2)}) async-start(bf16[8,512,256]{2,1,0:T(8,128)(2,1)} %stack.2), calls=%async_computation | async-start | bytes 4194304 | tf_op jit(solution)/shard_map/all_to_all | solution.py:14
  26.2 0.7 all-gather.5.cloned.1.call-update
  27.0 0.8 dynamic-slice
  27.7 0.8 compare_and_fusion
  28.5 0.6 gather_fusion
  29.6 122.8 %psum.56 = bf16[16,256]{1,0:T(8,128)(2,1)S(1)} all-reduce(f32[16,256]{1,0:T(8,128)S(1)} %fusion.29), channel_id=1, replica_groups=mesh['src'=4,'seq'=8,'head'=16] {'seq'}, use_global_device_ids=true, to_apply=%region_2.4 | all-reduce | flops 4096 | bytes 24576 | tf_op jit(solution)/shard_map/psum | solution.py:56
  152.5 66.7 %all-gather.3.cloned.1.call-done = bf16[1024,4096]{1,0:T(8,128)(2,1)} async-done(((bf16[1024,256]{1,0:T(8,128)(2,1)}), bf16[1024,4096]{1,0:T(8,128)(2,1)}) %all-gather.3.cloned.1.call-update) | async-done | bytes 8388624 | tf_op jit(solution)/shard_map/all_gather | solution.py:35
  219.2 5.1 fusion
  224.3 6.2 fusion.10
  230.8 30.1 %pmax.14 = f32[16,4]{0,1:T(4,128)S(1)} all-reduce(f32[16,4]{0,1:T(4,128)S(1)} %get-tuple-element.23), channel_id=1, replica_groups=mesh['src'=4,'seq'=8,'head'=16] {'seq'}, use_global_device_ids=true, to_apply=%region_4.6 | all-reduce | flops 64 | bytes 512 | tf_op jit(solution)/shard_map/pmax | solution.py:64
  261.1 28.3 %all-gather.5.cloned.1.call-done = bf16[4096,256]{1,0:T(8,128)(2,1)} async-done(((bf16[512,256]{1,0:T(8,128)(2,1)}), bf16[4096,256]{1,0:T(8,128)(2,1)}) %all-gather.5.cloned.1.call-update) | async-done | bytes 2097168 | tf_op jit(solution)/shard_map/all_gather | solution.py:39
  289.4 6.6 %fusion.7 = bf16[1024,256]{0,1:T(8,128)(2,1)S(1)} fusion(bf16[4096,256]{1,0:T(8,128)(2,1)} %all-gather.5.cloned.1.call-done, bf16[1024,4096]{1,0:T(8,128)(2,1)} %all-gather.3.cloned.1.call-done, f32[4096]{0:T(1024)S(1)} %copy-done.5, f32[1024]{0:T(1024)S(1)} %add_rsqrt_fusion), kind=kOutput, calls=%fused_computation.9 | convolution fusion | flops 2164523008 | bytes 11030528 | tf_op jit(solution)/shard_map/dot_general | solution.py:44
  296.3 34.6 %all-reduce.1 = (f32[16,4,64]{2,0,1:T(8,128)S(1)}, f32[16,4]{0,1:T(4,128)S(1)}) all-reduce(f32[16,4,64]{2,0,1:T(8,128)S(1)} %fusion.16, f32[16,4]{0,1:T(4,128)S(1)} %get-tuple-element.13), channel_id=1, replica_groups=mesh['src'=4,'seq'=8,'head'=16] {'seq'}, use_global_device_ids=true, to_apply=%region_5.7 | all-reduce | flops 4160 | bytes 33280 | tf_op jit(solution)/shard_map/psum | solution.py:66
  331.3 63.8 %psum.59 = bf16[16,512]{1,0:T(8,128)(2,1)S(1)} all-reduce(bf16[16,512]{1,0:T(8,128)(2,1)S(1)} %convolution_convert_fusion.1), channel_id=1, replica_groups=mesh['src'=4,'seq'=8,'head'=16] {'head'}, use_global_device_ids=true, to_apply=%region_8.10 | all-reduce | flops 8192 | bytes 32768 | tf_op jit(solution)/shard_map/psum | solution.py:70
  395.0 35.9 %all_gather.14 = bf16[16,4096]{1,0:T(8,128)(2,1)S(1)} all-gather(bf16[16,512]{1,0:T(8,128)(2,1)S(1)} %psum.59), channel_id=1, replica_groups=mesh['src'=4,'seq'=8,'head'=16] {'seq'}, dimensions={1}, use_global_device_ids=true | all-gather | bytes 147456 | tf_op jit(solution)/shard_map/all_gather | solution.py:71
  431.0 0.6 gather_fusion.1
  432.1 33.7 %psum.60 = bf16[16,256]{1,0:T(8,128)(2,1)S(1)} all-reduce(f32[16,256]{1,0:T(8,128)S(1)} %fusion.31), channel_id=1, replica_groups=mesh['src'=4,'seq'=8,'head'=16] {'seq'}, use_global_device_ids=true, to_apply=%region_10.12 | all-reduce | flops 4096 | bytes 24576 | tf_op jit(solution)/shard_map/psum | solution.py:56
  466.1 20.0 %pmax.15 = f32[16,4]{0,1:T(4,128)S(1)} all-reduce(f32[16,4]{0,1:T(4,128)S(1)} %get-tuple-element.25), channel_id=1, replica_groups=mesh['src'=4,'seq'=8,'head'=16] {'seq'}, use_global_device_ids=true, to_apply=%region_12.14 | all-reduce | flops 64 | bytes 512 | tf_op jit(solution)/shard_map/pmax | solution.py:64
  486.6 35.0 %all-reduce = (f32[16,4,64]{2,0,1:T(8,128)S(1)}, f32[16,4]{0,1:T(4,128)S(1)}) all-reduce(f32[16,4,64]{2,0,1:T(8,128)S(1)} %fusion.15, f32[16,4]{0,1:T(4,128)S(1)} %get-tuple-element.7), channel_id=1, replica_groups=mesh['src'=4,'seq'=8,'head'=16] {'seq'}, use_global_device_ids=true, to_apply=%region_13.15 | all-reduce | flops 4160 | bytes 33280 | tf_op jit(solution)/shard_map/psum | solution.py:66
  521.9 60.4 %psum.63 = bf16[16,512]{1,0:T(8,128)(2,1)S(1)} all-reduce(bf16[16,512]{1,0:T(8,128)(2,1)S(1)} %convolution_convert_fusion), channel_id=1, replica_groups=mesh['src'=4,'seq'=8,'head'=16] {'head'}, use_global_device_ids=true, to_apply=%region_16.18 | all-reduce | flops 8192 | bytes 32768 | tf_op jit(solution)/shard_map/psum | solution.py:70
  582.2 35.7 %all_gather.15 = bf16[16,4096]{1,0:T(8,128)(2,1)S(1)} all-gather(bf16[16,512]{1,0:T(8,128)(2,1)S(1)} %psum.63), channel_id=1, replica_groups=mesh['src'=4,'seq'=8,'head'=16] {'seq'}, dimensions={1}, use_global_device_ids=true | all-gather | bytes 147456 | tf_op jit(solution)/shard_map/all_gather | solution.py:71
  617.9 0.8 convert_add_fusion
  (43 shorter events, 3.3 us)
Async XLA Ops:
  7.2 21.3 %copy-start = (f32[16,4096]{1,0:T(8,128)S(1)}, f32[16,4096]{1,0:T(8,128)}, u32[]{:S(2)}) copy-start(f32[16,4096]{1,0:T(8,128)} %param.19) | copy-start | bytes 786436
  7.2 22.0 %copy-start.3 = (bf16[2,16,4096]{2,1,0:T(8,128)(2,1)S(1)}, bf16[2,16,4096]{2,1,0:T(8,128)(2,1)}, u32[]{:S(2)}) copy-start(bf16[2,16,4096]{2,1,0:T(8,128)(2,1)} %param.21) | copy-start | bytes 786436
  7.2 22.2 %copy-start.1 = (bf16[512,256]{1,0:T(8,128)(2,1)S(1)}, bf16[512,256]{1,0:T(8,128)(2,1)}, u32[]{:S(2)}) copy-start(bf16[512,256]{1,0:T(8,128)(2,1)} %param.16) | copy-start | bytes 786436
  7.2 212.0 %all-gather.3.cloned.1.call-start = ((), (), s32[]{:S(2)}) async-start(), calls=%async_computation.1 | async-start | bytes 8912896 | tf_op jit(solution)/shard_map/all_gather | solution.py:35
  10.3 214.0 %copy-start.5 = (f32[4096]{0:T(1024)S(1)}, f32[4096]{0:T(1024)}, u32[]{:S(2)}) copy-start(f32[4096]{0:T(1024)} %param.13) | copy-start | bytes 49156
  10.3 213.9 %all-to-all-start = ((bf16[8,512,256]{2,1,0:T(8,128)(2,1)}), bf16[8,512,256]{2,1,0:T(8,128)(2,1)S(1)}, u32[]{:S(2)}, u32[]{:S(2)}) async-start(bf16[8,512,256]{2,1,0:T(8,128)(2,1)} %stack.2), calls=%async_computation | async-start | bytes 4194304 | tf_op jit(solution)/shard_map/all_to_all | solution.py:14
  26.2 263.2 %all-gather.5.cloned.1.call-start = ((), (), s32[]{:S(2)}) async-start(), calls=%async_computation.2 | async-start | bytes 2359296 | tf_op jit(solution)/shard_map/all_gather | solution.py:39
  261.0 70.1 %copy-start.2 = (bf16[256,512]{1,0:T(8,128)(2,1)S(1)}, bf16[256,512]{1,0:T(8,128)(2,1)}, u32[]{:S(2)}) copy-start(bf16[256,512]{1,0:T(8,128)(2,1)} %param.17) | copy-start | bytes 786436
  261.1 170.6 %copy-start.4 = (bf16[2,16,4096]{2,1,0:T(8,128)(2,1)S(1)}, bf16[2,16,4096]{2,1,0:T(8,128)(2,1)}, u32[]{:S(2)}) copy-start(bf16[2,16,4096]{2,1,0:T(8,128)(2,1)} %param.21) | copy-start | bytes 786436
Sparse Core Ops, SparseCore 0:
  10.0 209.1 all-gather.2
  221.3 68.0 all-gather.4
